TPU v7x, 512 devices: a whole 4x4x16 slice. The times are simulated.
512 devices in a mesh: frames: 64 (over z, y), strips: 8 (over x, core).
Axes of the slice: x: 4, y: 4, z: 16, core: 2. Of those that a mesh axis runs over, the one named last changes fastest.
Arguments:
- raw_frames: bfloat16 [4096, 512, 512], P('frames', 'strips'), may hold values from -24 to 24
- dark_frame: float32 [512, 512], P('strips'), may hold values from -6 to 6
- dead_mask: int32 [512, 512], P('strips'), may hold values 0 or 1
- frame_group: int32 [4096], P('frames'), may hold values from 0 to 7
- prior_sigma: float32 [128], replicated, may hold values from 0.2 to 0.5
- start_rotation: float32 [128, 128], replicated, as said below
- basis: bfloat16 [262144, 128], P(('strips', 'frames')), may hold values from -0.01171875 to 0.01171875
Outputs:
- new_basis: bfloat16 [262144, 128], P(('strips', 'frames'))
- new_coeffs: float32 [4096, 128], P('frames')
- new_sigma: float32 [128], replicated
Inputs may be any that keep to these rules, and one draw needn't show every extreme that they name: start_rotation is nonsingular.
All inputs are finite; a program needn't handle non-finite values. No bound on the sum of `dead_mask` on one device may be relied on, other than what follows from the above.
Results may differ from a plain program's by a relative error of at most 0.0071.
Values may be sent and summed in bfloat16 or wider, within the bound.
A program may use at most 64 MiB of HBM per device.

v0:
```python
import jax
import jax.numpy as jnp
from jax import lax
from jax.sharding import PartitionSpec as P

GROUPS = 8
ITERS = 4
BLUR_TAPS = (1.0 / 64, 6.0 / 64, 15.0 / 64, 20.0 / 64, 15.0 / 64, 6.0 / 64, 1.0 / 64)
DECAY_RATE = 0.7


def extended(shard, sides, width):
    for axis, dim in sides:
        size, length = (lax.axis_size(axis), shard.shape[dim])
        up = [(i, (i + 1) % size) for i in range(size - 1)]
        down = [(j, i) for i, j in up]
        last = lax.slice_in_dim(shard, length - width, length, axis=dim)
        first = lax.slice_in_dim(shard, 0, width, axis=dim)
        before = lax.ppermute(last, axis, up)
        after = lax.ppermute(first, axis, down)
        shard = jnp.concatenate([before, shard, after], axis=dim)
    return shard


def orthonormalize(product):
    normal = jnp.dot(product.T, product, precision=lax.Precision.HIGHEST)
    factor = jnp.linalg.cholesky(normal)
    return lax.linalg.triangular_solve(
        factor, product, left_side=False, lower=True, transpose_a=True
    )


def body(raw_frames, dark_frame, dead_mask, frame_group, prior_sigma, start_rotation, basis):
    frame_count, strip_rows, columns = raw_frames.shape
    corrected = (
        (raw_frames.astype(jnp.float32) - dark_frame) * (1 - dead_mask).astype(jnp.float32)
    ).astype(jnp.bfloat16)
    position = jnp.arange(columns)
    offsets = position[None, :] - position[:, None]
    banded = jnp.zeros((columns, columns), jnp.float32)
    for shift_by in range(-3, 4):
        banded = banded + jnp.where(offsets == shift_by, BLUR_TAPS[shift_by + 3], 0.0)
    banded = banded.astype(jnp.bfloat16)
    column_blur = jnp.dot(
        corrected.reshape(frame_count * strip_rows, columns),
        banded,
        preferred_element_type=jnp.float32,
    )
    column_blur = column_blur.reshape(frame_count, strip_rows, columns)
    padded = extended(column_blur, (("strips", 1),), 3)
    row_blur = BLUR_TAPS[0] * padded[:, 0:strip_rows, :]
    for offset in range(1, 7):
        row_blur = row_blur + BLUR_TAPS[offset] * padded[:, offset : offset + strip_rows, :]
    frame_weight = jnp.power(
        jnp.float32(DECAY_RATE), (GROUPS - 1 - frame_group).astype(jnp.float32)
    )
    weighted = (
        (frame_weight[:, None, None] * row_blur)
        .astype(jnp.bfloat16)
        .reshape(frame_count, strip_rows * columns)
    )
    partial_value = jnp.dot(
        weighted,
        lax.all_gather(basis, "frames", axis=0, tiled=True),
        preferred_element_type=jnp.float32,
    )
    coeffs = lax.psum(partial_value, "strips")
    total_frames = frame_count * lax.axis_size("frames")
    local_gram = jnp.dot(coeffs.T, coeffs, precision=lax.Precision.HIGHEST)
    summed_gram = lax.psum(local_gram, "frames")
    gram = jnp.diag(prior_sigma * prior_sigma) + summed_gram / total_frames
    rotation = start_rotation
    for step in range(ITERS):
        rotation = orthonormalize(jnp.dot(gram, rotation, precision=lax.Precision.HIGHEST))
    new_coeffs = jnp.dot(coeffs, rotation, precision=lax.Precision.HIGHEST)
    new_basis = jnp.dot(
        basis.astype(jnp.float32), rotation, precision=lax.Precision.HIGHEST
    ).astype(jnp.bfloat16)
    curved = jnp.dot(gram, rotation, precision=lax.Precision.HIGHEST)
    new_sigma = jnp.sqrt(jnp.sum(rotation * curved, axis=0))
    return (new_basis, new_coeffs, new_sigma)


def solution(mesh):
    placed = (
        P("frames", "strips", None),
        P("strips", None),
        P("strips", None),
        P("frames"),
        P(),
        P(),
        P(("strips", "frames"), None),
    )
    return jax.shard_map(
        body,
        mesh=mesh,
        in_specs=placed,
        out_specs=(P(("strips", "frames"), None), P("frames", None), P()),
        check_vma=False,
    )
```

profile of v0, /device:TPU:2, one launch (start us, length us, event | category | flops | bytes accessed | tf_op | source)
XLA Modules:
  0.0 562.9 jit_solution(2204300600447689643)
XLA Ops:
  7.2 0.7 all-gather.2.cloned.1.call-update
  8.0 0.9 subtract_convert_fusion
  8.9 4.7 fusion.18
  13.6 0.2 fusion.85
  13.9 1.9 collective-permute-start
  15.8 3.6 collective-permute-start.1
  19.5 4.9 collective-permute-done
  24.4 1.8 collective-permute-done.1
  26.1 8.9 %fusion.5 = bf16[64,64,512]{2,1,0:T(8,128)(2,1)S(1)} fusion(f32[64,64,512]{2,1,0:T(8,128)S(1)} %fusion.18, f32[64,3,512]{2,1,0:T(4,128)S(1)} %collective-permute-done.1, f32[64,3,512]{2,1,0:T(4,128)S(1)} %collective-permute-done, f32[64]{0:T(128)S(1)} %convert_power_fusion), kind=kLoop, calls=%fused_computation.13 | loop fusion | flops 44040192 | bytes 13369600 | tf_op jit(solution)/shard_map/convert_element_type | solution.py:59
  35.0 4.5 copy.15
  39.6 132.9 %all-gather.2.cloned.1.call-done = bf16[32768,128]{1,0:T(8,128)(2,1)} async-done(((bf16[512,128]{1,0:T(8,128)(2,1)}), bf16[32768,128]{1,0:T(8,128)(2,1)}) %all-gather.2.cloned.1.call-update) | async-done | bytes 8388624 | tf_op jit(solution)/shard_map/all_gather | solution.py:64
  172.4 6.3 %fusion.86 = f32[64,128]{1,0:T(8,128)S(1)} fusion(bf16[64,32768]{1,0:T(8,128)(2,1)} %bitcast.76, bf16[32768,128]{1,0:T(8,128)(2,1)} %all-gather.2.cloned.1.call-done), kind=kOutput, calls=%fused_computation.116 | convolution fusion | flops 536870912 | bytes 12615680 | tf_op jit(solution)/shard_map/dot_general | solution.py:62
  178.7 20.7 %psum.14 = f32[64,128]{1,0:T(8,128)S(1)} all-reduce(f32[64,128]{1,0:T(8,128)S(1)} %fusion.86), channel_id=1, replica_groups=mesh['frames'=64,'strips'=8] {'strips'}, use_global_device_ids=true, to_apply=%region_0.1 | all-reduce | flops 8192 | bytes 65536 | tf_op jit(solution)/shard_map/psum | solution.py:67
  199.4 0.9 fusion.87
  200.4 253.0 %all-reduce.2.cloned.1.call-done = f32[128,128]{1,0:T(8,128)} async-done(((f32[128,128]{1,0:T(8,128)}), f32[128,128]{1,0:T(8,128)}) %all-reduce.2.cloned.1.call-update) | async-done | bytes 65552 | tf_op jit(solution)/shard_map/psum | solution.py:70
  453.4 1.1 fusion.83
  454.5 0.3 fusion.88
  454.9 11.7 %cholesky.74 = f32[128,128]{1,0:T(8,128)S(1)} custom-call(f32[128,128]{1,0:T(8,128)S(1)} %fusion.55), custom_call_target="Cholesky" | custom-call | tf_op jit(solution)/shard_map/jit(cholesky)/cholesky | solution.py:27
  466.6 0.6 compare_reduce_fusion.3
  467.3 0.7 fusion.44
  468.0 9.8 %custom-call.8 = f32[1,128,128]{1,2,0:T(8,128)S(1)} custom-call(f32[1,128,128]{2,1,0:T(8,128)S(1)} %fusion.44), custom_call_target="InvertDiagBlocksLowerTriangular" | custom-call | tf_op jit(solution)/shard_map/triangular_solve/custom-call.0 | solution.py:28
  477.8 0.3 convolution_bitcast_fusion.3
  478.1 1.1 fusion.81
  479.2 0.3 fusion.89
  479.6 11.7 %cholesky.85 = f32[128,128]{1,0:T(8,128)S(1)} custom-call(f32[128,128]{1,0:T(8,128)S(1)} %fusion.53), custom_call_target="Cholesky" | custom-call | tf_op jit(solution)/shard_map/jit(cholesky)/cholesky | solution.py:27
  491.4 0.6 compare_reduce_fusion.2
  492.0 0.7 fusion.45
  492.7 10.0 %custom-call.9 = f32[1,128,128]{1,2,0:T(8,128)S(1)} custom-call(f32[1,128,128]{2,1,0:T(8,128)S(1)} %fusion.45), custom_call_target="InvertDiagBlocksLowerTriangular" | custom-call | tf_op jit(solution)/shard_map/triangular_solve/custom-call.0 | solution.py:28
  502.7 0.3 convolution_bitcast_fusion.2
  503.0 1.1 fusion.79
  504.1 0.3 fusion.90
  504.5 11.7 %cholesky.96 = f32[128,128]{1,0:T(8,128)S(1)} custom-call(f32[128,128]{1,0:T(8,128)S(1)} %fusion.51), custom_call_target="Cholesky" | custom-call | tf_op jit(solution)/shard_map/jit(cholesky)/cholesky | solution.py:27
  516.3 0.6 compare_reduce_fusion.1
  516.9 0.7 fusion.46
  517.6 9.8 %custom-call.10 = f32[1,128,128]{1,2,0:T(8,128)S(1)} custom-call(f32[1,128,128]{2,1,0:T(8,128)S(1)} %fusion.46), custom_call_target="InvertDiagBlocksLowerTriangular" | custom-call | tf_op jit(solution)/shard_map/triangular_solve/custom-call.0 | solution.py:28
  527.4 0.3 convolution_bitcast_fusion.1
  527.7 1.1 fusion.77
  528.8 0.3 fusion.91
  529.2 11.7 %cholesky.107 = f32[128,128]{1,0:T(8,128)S(1)} custom-call(f32[128,128]{1,0:T(8,128)S(1)} %fusion.49), custom_call_target="Cholesky" | custom-call | tf_op jit(solution)/shard_map/jit(cholesky)/cholesky | solution.py:27
  541.0 0.6 compare_reduce_fusion
  541.6 0.7 fusion.47
  542.3 10.0 %custom-call.11 = f32[1,128,128]{1,2,0:T(8,128)S(1)} custom-call(f32[1,128,128]{2,1,0:T(8,128)S(1)} %fusion.47), custom_call_target="InvertDiagBlocksLowerTriangular" | custom-call | tf_op jit(solution)/shard_map/triangular_solve/custom-call.0 | solution.py:28
  552.3 0.2 convolution_bitcast_fusion
  552.5 0.8 fusion.92
  553.3 0.3 fusion.21
  553.6 1.1 fusion.22
  554.7 0.5 sqrt.3
  555.3 0.8 copy.14
  (25 shorter events, 0.7 us)
Async XLA Ops:
  7.2 446.2 %copy-start = (f32[128,128]{1,0:T(8,128)S(1)}, f32[128,128]{1,0:T(8,128)}, u32[]{:S(2)}) copy-start(f32[128,128]{1,0:T(8,128)} %param.15) | copy-start | bytes 196612
  7.2 165.3 %all-gather.2.cloned.1.call-start = ((), (), s32[]{:S(2)}) async-start(), calls=%async_computation | async-start | bytes 8519680 | tf_op jit(solution)/shard_map/all_gather | solution.py:64
  7.9 445.5 %all-reduce.2.cloned.1.call-start = ((), (), s32[]{:S(2)}) async-start(), calls=%async_computation.1 | async-start | bytes 131072 | tf_op jit(solution)/shard_map/psum | solution.py:70
  8.9 10.6 %copy-start.2 = (s32[64]{0:T(128)S(1)}, s32[64]{0:T(128)}, u32[]{:S(2)}) copy-start(s32[64]{0:T(128)} %param.13) | copy-start | bytes 772
  13.9 10.5 %collective-permute-start = (f32[64,3,512]{2,1,0:T(4,128)S(1)}, f32[64,3,512]{2,1,0:T(4,128)S(1)}, u32[]{:S(2)}, u32[]{:S(2)}) collective-permute-start(f32[64,3,512]{2,1,0:T(4,128)S(1)} %get-tuple-element.8), channel_id=1, source_target_pairs={{0,1},{1,2},{2,3},{3,4},{4,5},{5,6},{6,7},{8,9},{9,10},{10,11},{11... | collective-permute-start | bytes 1179656 | tf_op jit(solution)/shard_map/ppermute | solution.py:19
  15.8 10.3 %collective-permute-start.1 = (f32[64,3,512]{2,1,0:T(4,128)S(1)}, f32[64,3,512]{2,1,0:T(4,128)S(1)}, u32[]{:S(2)}, u32[]{:S(2)}) collective-permute-start(f32[64,3,512]{2,1,0:T(4,128)S(1)} %get-tuple-element.9), channel_id=1, source_target_pairs={{1,0},{2,1},{3,2},{4,3},{5,4},{6,5},{7,6},{9,8},{10,9},{11,10},{12... | collective-permute-start | bytes 1179656 | tf_op jit(solution)/shard_map/ppermute | solution.py:20
  172.4 27.9 %copy-start.3 = (f32[128]{0:T(128)S(1)}, f32[128]{0:T(128)}, u32[]{:S(2)}) copy-start(f32[128]{0:T(128)} %param.14) | copy-start | bytes 1540
  172.4 380.9 %copy-start.1 = (bf16[512,128]{1,0:T(8,128)(2,1)S(1)}, bf16[512,128]{1,0:T(8,128)(2,1)}, u32[]{:S(2)}) copy-start(bf16[512,128]{1,0:T(8,128)(2,1)} %param.16) | copy-start | bytes 393220
Sparse Core Ops, SparseCore 0:
  11.0 161.4 all-gather.1
  200.5 252.8 all-reduce.1
where the time goes:
time: 563 us
  waiting for transfers between devices  393 us (70%)
  other arithmetic  102 us (18%)
  matrix products  20.9 us (4%)
  blocking collectives  20.7 us (4%)
  between operations  14.3 us (3%)
  local copies, waits for them, and re-layouts  6.45 us (1%)
  starting transfers between devices  5.64 us (1%)
    psum x1, waiting for transfers between devices, body(): summed_gram = lax.psum(local_gram, 'frames')  253 us
    all_gather x1, waiting for transfers between devices, body(): lax.all_gather(basis, 'frames', axis=0, tiled=True)  133 us
    another operation x12, other arithmetic, orthonormalize(): factor = jnp.linalg.cholesky(normal)  49.6 us
    another operation x8, other arithmetic, orthonormalize(): lax.linalg.triangular_solve(factor, product, left_side=False, lower=True,...  42.2 us
    psum x1, blocking collectives, body(): coeffs = lax.psum(partial_value, 'strips')  20.7 us
  transfers between devices with their start and end apart: 4, of which 4 were waited for; matrix products, arithmetic and copies ran while one was open for 3% of the time, Pallas kernels for 0%

commit v1 on v0

--- a/solution.py
+++ b/solution.py
@@ -59,10 +59,14 @@
         .astype(jnp.bfloat16)
         .reshape(frame_count, strip_rows * columns)
     )
+
+    def finish_the_goods(s0, ax_name):
+        base_arr = lax.axis_size(ax_name)
+        x_now = jnp.concatenate(base_arr * [s0], axis=0)
+        return lax.all_to_all(x_now, axis_name=ax_name, split_axis=0, concat_axis=0, tiled=True)
+
     partial_value = jnp.dot(
-        weighted,
-        lax.all_gather(basis, "frames", axis=0, tiled=True),
-        preferred_element_type=jnp.float32,
+        weighted, finish_the_goods(basis, "frames"), preferred_element_type=jnp.float32
     )
     coeffs = lax.psum(partial_value, "strips")
     total_frames = frame_count * lax.axis_size("frames")

time: 563 us -> 828 us (1.47)
  waiting for transfers between devices: 393 us -> 600 us
  local copies, waits for them, and re-layouts: 6.45 us -> 35.4 us
  starting transfers between devices: 5.64 us -> 25.3 us
    all_to_all x0 -> x1, waiting for transfers between devices: none -> 343 us  [finish_the_goods(): lax.all_to_all(x_now, axis_name=ax_name, split_axis=0, concat_axis=0, til...]
    all_gather x1 -> x0, waiting for transfers between devices: 133 us -> none  [body(): lax.all_gather(basis, 'frames', axis=0, tiled=True)]
    unnamed x10 -> x78, local copies, waits for them, and re-layouts: 5.33 us -> 34.2 us
    all_to_all x0 -> x1, starting transfers between devices: none -> 19.1 us  [finish_the_goods(): lax.all_to_all(x_now, axis_name=ax_name, split_axis=0, concat_axis=0, til...]
  transfers between devices with their start and end apart: 4 -> 4, of which waited for: 4 -> 4; matrix products, arithmetic and copies ran while one was open for 3% -> 2% of each run, Pallas kernels for 0% -> 0%
where the time goes in v1:
time: 828 us; the launch traced here: 823 us
  waiting for transfers between devices  600 us (72%)
  other arithmetic  102 us (12%)
  local copies, waits for them, and re-layouts  35.4 us (4%)
  starting transfers between devices  25.3 us (3%)
  matrix products  24.2 us (3%)
  blocking collectives  20.8 us (3%)
  between operations  15 us (2%)
    all_to_all x1, waiting for transfers between devices, finish_the_goods(): lax.all_to_all(x_now, axis_name=ax_name, split_axis=0, concat_axis=0, til...  343 us
    psum x1, waiting for transfers between devices, body(): summed_gram = lax.psum(local_gram, 'frames')  251 us
    another operation x12, other arithmetic, orthonormalize(): factor = jnp.linalg.cholesky(normal)  49.6 us
    another operation x8, other arithmetic, orthonormalize(): lax.linalg.triangular_solve(factor, product, left_side=False, lower=True,...  42.3 us
    unnamed x78, local copies, waits for them, and re-layouts  34.2 us
    psum x1, blocking collectives, body(): coeffs = lax.psum(partial_value, 'strips')  20.8 us
    all_to_all x1, starting transfers between devices, finish_the_goods(): lax.all_to_all(x_now, axis_name=ax_name, split_axis=0, concat_axis=0, til...  19.1 us
  transfers between devices with their start and end apart: 4, of which 4 were waited for; matrix products, arithmetic and copies ran while one was open for 2% of the time, Pallas kernels for 0%

profile of v1, /device:TPU:2, one launch (start us, length us, event | category | flops | bytes accessed | tf_op | source)
XLA Modules:
  0.0 822.6 jit_solution(11574078588855065247)
XLA Ops:
  7.2 1.0 constant_dynamic-update-slice_fusion.63
  8.2 0.9 constant_dynamic-update-slice_fusion.62
  9.1 0.9 constant_dynamic-update-slice_fusion.61
  10.0 0.9 constant_dynamic-update-slice_fusion.60
  11.0 0.9 constant_dynamic-update-slice_fusion.59
  11.9 0.9 constant_dynamic-update-slice_fusion.58
  12.8 0.9 constant_dynamic-update-slice_fusion.57
  13.7 0.9 constant_dynamic-update-slice_fusion.56
  14.7 0.9 constant_dynamic-update-slice_fusion.55
  15.6 0.9 constant_dynamic-update-slice_fusion.54
  16.5 0.9 constant_dynamic-update-slice_fusion.53
  17.4 0.9 constant_dynamic-update-slice_fusion.52
  18.4 0.9 constant_dynamic-update-slice_fusion.51
  20.2 0.9 constant_dynamic-update-slice_fusion.49
  22.1 0.9 constant_dynamic-update-slice_fusion.47
  23.9 0.9 constant_dynamic-update-slice_fusion.45
  24.9 0.9 constant_dynamic-update-slice_fusion.44
  26.7 0.9 constant_dynamic-update-slice_fusion.42
  28.6 0.9 constant_dynamic-update-slice_fusion.40
  30.4 0.9 constant_dynamic-update-slice_fusion.38
  31.4 0.9 constant_dynamic-update-slice_fusion.37
  33.2 0.9 constant_dynamic-update-slice_fusion.35
  35.1 0.9 constant_dynamic-update-slice_fusion.33
  37.8 3.2 copy-done.2
  41.0 19.1 %all-to-all-start = ((bf16[64,512,128]{2,1,0:T(8,128)(2,1)}), bf16[64,512,128]{2,1,0:T(8,128)(2,1)}, u32[]{:S(2)}, u32[]{:S(2)}) async-start(bf16[64,512,128]{2,1,0:T(8,128)(2,1)} %bitcast.76), calls=%async_computation | async-start | bytes 16777216 | tf_op jit(solution)/shard_map/all_to_all | solution.py:66
  60.3 4.7 fusion.18
  65.2 1.9 collective-permute-start
  67.2 4.2 collective-permute-start.1
  71.4 4.4 collective-permute-done
  75.7 1.8 collective-permute-done.1
  77.5 9.7 %fusion.5 = bf16[64,64,512]{2,1,0:T(8,128)(2,1)} fusion(f32[64,64,512]{2,1,0:T(8,128)S(1)} %fusion.18, f32[64,3,512]{2,1,0:T(4,128)S(1)} %collective-permute-done.1, f32[64,3,512]{2,1,0:T(4,128)S(1)} %collective-permute-done, f32[64]{0:T(128)S(1)} %convert_power_fusion), kind=kLoop, calls=%fused_computation.13 | loop fusion | flops 44040192 | bytes 13369600 | tf_op jit(solution)/shard_map/convert_element_type | solution.py:59
  87.2 342.7 %all-to-all-done = bf16[64,512,128]{2,1,0:T(8,128)(2,1)} async-done(((bf16[64,512,128]{2,1,0:T(8,128)(2,1)}), bf16[64,512,128]{2,1,0:T(8,128)(2,1)}, u32[]{:S(2)}, u32[]{:S(2)}) %all-to-all-start) | async-done | bytes 8388640 | tf_op jit(solution)/shard_map/all_to_all | solution.py:66
  429.9 9.6 %fusion.25 = f32[64,128]{1,0:T(8,128)S(1)} fusion(bf16[64,512,128]{2,1,0:T(8,128)(2,1)} %all-to-all-done, bf16[64,64,512]{2,1,0:T(8,128)(2,1)} %fusion.5), kind=kOutput, calls=%fused_computation.42 | convolution fusion | flops 536870912 | bytes 12615680 | tf_op jit(solution)/shard_map/dot_general | solution.py:68
  439.6 20.8 %psum.14 = f32[64,128]{1,0:T(8,128)S(1)} all-reduce(f32[64,128]{1,0:T(8,128)S(1)} %fusion.25), channel_id=1, replica_groups=mesh['frames'=64,'strips'=8] {'strips'}, use_global_device_ids=true, to_apply=%region_0.1 | all-reduce | flops 8192 | bytes 65536 | tf_op jit(solution)/shard_map/psum | solution.py:71
  461.3 251.5 %all-reduce.2.cloned.1.call-done = f32[128,128]{1,0:T(8,128)} async-done(((f32[128,128]{1,0:T(8,128)}), f32[128,128]{1,0:T(8,128)}) %all-reduce.2.cloned.1.call-update) | async-done | bytes 65552 | tf_op jit(solution)/shard_map/psum | solution.py:74
  712.8 1.1 fusion.88
  714.3 11.7 %cholesky.74 = f32[128,128]{1,0:T(8,128)S(1)} custom-call(f32[128,128]{1,0:T(8,128)S(1)} %fusion.60), custom_call_target="Cholesky" | custom-call | tf_op jit(solution)/shard_map/jit(cholesky)/cholesky | solution.py:27
  727.4 9.8 %custom-call.8 = f32[1,128,128]{1,2,0:T(8,128)S(1)} custom-call(f32[1,128,128]{2,1,0:T(8,128)S(1)} %fusion.49), custom_call_target="InvertDiagBlocksLowerTriangular" | custom-call | tf_op jit(solution)/shard_map/triangular_solve/custom-call.0 | solution.py:28
  737.5 1.1 fusion.86
  739.0 11.7 %cholesky.85 = f32[128,128]{1,0:T(8,128)S(1)} custom-call(f32[128,128]{1,0:T(8,128)S(1)} %fusion.58), custom_call_target="Cholesky" | custom-call | tf_op jit(solution)/shard_map/jit(cholesky)/cholesky | solution.py:27
  752.1 10.0 %custom-call.9 = f32[1,128,128]{1,2,0:T(8,128)S(1)} custom-call(f32[1,128,128]{2,1,0:T(8,128)S(1)} %fusion.50), custom_call_target="InvertDiagBlocksLowerTriangular" | custom-call | tf_op jit(solution)/shard_map/triangular_solve/custom-call.0 | solution.py:28
  762.4 1.1 fusion.84
  763.9 11.7 %cholesky.96 = f32[128,128]{1,0:T(8,128)S(1)} custom-call(f32[128,128]{1,0:T(8,128)S(1)} %fusion.56), custom_call_target="Cholesky" | custom-call | tf_op jit(solution)/shard_map/jit(cholesky)/cholesky | solution.py:27
  777.0 9.8 %custom-call.10 = f32[1,128,128]{1,2,0:T(8,128)S(1)} custom-call(f32[1,128,128]{2,1,0:T(8,128)S(1)} %fusion.51), custom_call_target="InvertDiagBlocksLowerTriangular" | custom-call | tf_op jit(solution)/shard_map/triangular_solve/custom-call.0 | solution.py:28
  787.1 1.1 fusion.82
  788.6 11.7 %cholesky.107 = f32[128,128]{1,0:T(8,128)S(1)} custom-call(f32[128,128]{1,0:T(8,128)S(1)} %fusion.54), custom_call_target="Cholesky" | custom-call | tf_op jit(solution)/shard_map/jit(cholesky)/cholesky | solution.py:27
  801.7 10.0 %custom-call.11 = f32[1,128,128]{1,2,0:T(8,128)S(1)} custom-call(f32[1,128,128]{2,1,0:T(8,128)S(1)} %fusion.52), custom_call_target="InvertDiagBlocksLowerTriangular" | custom-call | tf_op jit(solution)/shard_map/triangular_solve/custom-call.0 | solution.py:28
  813.1 1.1 fusion.24
  (93 shorter events, 20.6 us)
Async XLA Ops:
  7.2 705.6 %copy-start = (f32[128,128]{1,0:T(8,128)S(1)}, f32[128,128]{1,0:T(8,128)}, u32[]{:S(2)}) copy-start(f32[128,128]{1,0:T(8,128)} %param.15) | copy-start | bytes 196612
  7.2 29.7 %copy-start.1 = (bf16[512,128]{1,0:T(8,128)(2,1)S(1)}, bf16[512,128]{1,0:T(8,128)(2,1)}, u32[]{:S(2)}) copy-start(bf16[512,128]{1,0:T(8,128)(2,1)} %param.16) | copy-start | bytes 393220
  37.8 3.2 copy-start.2
  41.0 19.2 %copy-start.3 = (s32[64,512]{1,0:T(8,128)S(1)}, s32[64,512]{1,0:T(8,128)}, u32[]{:S(2)}) copy-start(s32[64,512]{1,0:T(8,128)} %param.12) | copy-start | bytes 393220
  41.0 19.2 %copy-start.4 = (f32[64,512]{1,0:T(8,128)S(1)}, f32[64,512]{1,0:T(8,128)}, u32[]{:S(2)}) copy-start(f32[64,512]{1,0:T(8,128)} %param.11) | copy-start | bytes 393220
  41.0 388.9 %all-to-all-start = ((bf16[64,512,128]{2,1,0:T(8,128)(2,1)}), bf16[64,512,128]{2,1,0:T(8,128)(2,1)}, u32[]{:S(2)}, u32[]{:S(2)}) async-start(bf16[64,512,128]{2,1,0:T(8,128)(2,1)} %bitcast.76), calls=%async_computation | async-start | bytes 16777216 | tf_op jit(solution)/shard_map/all_to_all | solution.py:66
  60.2 652.7 %all-reduce.2.cloned.1.call-start = ((), (), s32[]{:S(2)}) async-start(), calls=%async_computation.1 | async-start | bytes 131072 | tf_op jit(solution)/shard_map/psum | solution.py:74
  60.2 11.1 %copy-start.5 = (s32[64]{0:T(128)S(1)}, s32[64]{0:T(128)}, u32[]{:S(2)}) copy-start(s32[64]{0:T(128)} %param.13) | copy-start | bytes 772
  65.2 10.5 %collective-permute-start = (f32[64,3,512]{2,1,0:T(4,128)S(1)}, f32[64,3,512]{2,1,0:T(4,128)S(1)}, u32[]{:S(2)}, u32[]{:S(2)}) collective-permute-start(f32[64,3,512]{2,1,0:T(4,128)S(1)} %get-tuple-element.8), channel_id=1, source_target_pairs={{0,1},{1,2},{2,3},{3,4},{4,5},{5,6},{6,7},{8,9},{9,10},{10,11},{11... | collective-permute-start | bytes 1179656 | tf_op jit(solution)/shard_map/ppermute | solution.py:19
  67.2 10.3 %collective-permute-start.1 = (f32[64,3,512]{2,1,0:T(4,128)S(1)}, f32[64,3,512]{2,1,0:T(4,128)S(1)}, u32[]{:S(2)}, u32[]{:S(2)}) collective-permute-start(f32[64,3,512]{2,1,0:T(4,128)S(1)} %get-tuple-element.9), channel_id=1, source_target_pairs={{1,0},{2,1},{3,2},{4,3},{5,4},{6,5},{7,6},{9,8},{10,9},{11,10},{12... | collective-permute-start | bytes 1179656 | tf_op jit(solution)/shard_map/ppermute | solution.py:20
  87.2 374.1 %copy-start.6 = (f32[128]{0:T(128)S(1)}, f32[128]{0:T(128)}, u32[]{:S(2)}) copy-start(f32[128]{0:T(128)} %param.14) | copy-start | bytes 1540
Sparse Core Ops, SparseCore 0:
  461.4 251.3 all-reduce.1
